TPU v7x, 768 devices: a whole 4x8x12 slice. The times are simulated.
768 devices in a mesh: elem: 96 (over y, z), face: 8 (over x, core).
Axes of the slice: x: 4, y: 8, z: 12, core: 2. Of those that a mesh axis runs over, the one named last changes fastest.
Arguments:
- vol_inverse: bfloat16 [3072, 320, 320], P(('elem', 'face')), may hold values from -0.3125 to 0.3125
- vol_from_trace: bfloat16 [3072, 320, 480], P(('elem', 'face')), may hold values from -0.25 to 0.25
- trace_from_vol: bfloat16 [3072, 480, 320], P(('elem', 'face')), may hold values from -0.25 to 0.25
- vol_residual: bfloat16 [3072, 320], P(('elem', 'face')), may hold values from -6 to 6
- face_ids: int32 [3072, 6], P(('elem', 'face')), may hold values from 0 to 9215, as said below
- trace_residual: float32 [9216, 80], P(('elem', 'face')), may hold values from -6 to 6
- stabilization: float32 [9216, 80], P(('elem', 'face')), may hold values from 1.5 to 4
Outputs:
- trace_update: float32 [9216, 80], P(('elem', 'face'))
- vol_update: float32 [3072, 320], P(('elem', 'face'))
Inputs may be any that keep to these rules, and one draw needn't show every extreme that they name: `face_ids`: owner group g holds elements g * 32 to (g + 1) * 32 - 1 and faces g * 96 to (g + 1) * 96 - 1. Every face is named by exactly two slots, and the 6 slots of one element name different faces. The slots of group g name faces of group g, or faces 0 to 31 of group (g - 1) mod 96; faces 0 to 31 of group g are named by one slot of group g and one slot of group (g + 1) mod 96; all other faces of group g are named by two slots of group g.
All inputs are finite; a program needn't handle non-finite values.
Results may differ from a plain program's by a relative error of at most 0.007.
Values may be sent and summed in bfloat16 or wider, within the bound.
A program may use at most 32 MiB of HBM per device.

v0:
```python
import jax
import jax.numpy as jnp
from jax import lax
from jax.sharding import PartitionSpec as P

SWEEPS = 5


exact_precision = lax.Precision.HIGHEST


def shifted(block, axis, distance):
    devices = range(lax.axis_size(axis))
    route = [((i - distance) % len(devices), i) for i in devices]
    return lax.ppermute(block, axis, route)


def local(
    vol_inverse,
    vol_from_trace,
    trace_from_vol,
    vol_residual,
    face_ids,
    trace_residual,
    stabilization,
):
    groups = lax.axis_size("elem")
    members = lax.axis_size("face")
    elem_count, side_count = face_ids.shape
    own_faces, trace_width = trace_residual.shape
    group_faces = own_faces * members
    border = elem_count * members
    slot_count = elem_count * side_count
    group_index = lax.axis_index("elem")
    lower_group = (group_index + groups - 1) % groups
    slot_ids = face_ids.reshape(slot_count)
    own_hits = (slot_ids - group_index * group_faces)[:, None] == lax.broadcasted_iota(
        jnp.int32, (slot_count, group_faces), 1
    )
    lower_hits = (slot_ids - lower_group * group_faces)[:, None] == lax.broadcasted_iota(
        jnp.int32, (slot_count, border), 1
    )
    own_float = own_hits.astype(jnp.float32)
    lower_float = lower_hits.astype(jnp.float32)
    own_half = own_hits.astype(jnp.bfloat16)
    lower_half = lower_hits.astype(jnp.bfloat16)

    def assemble(contrib):
        own_sum = jnp.einsum("sf,sw->fw", own_float, contrib, precision=exact_precision)
        lower_sum = jnp.einsum("sb,sw->bw", lower_float, contrib, precision=exact_precision)
        arrived = shifted(lower_sum, "elem", -1)
        partial_value = jnp.concatenate([own_sum[:border] + arrived, own_sum[border:]], axis=0)
        summed = lax.psum(partial_value, "face")
        return summed

    def distribute(lam_rows):
        upper_rows = shifted(lam_rows[:border], "elem", 1)
        slot_values = jnp.dot(own_half, lam_rows, preferred_element_type=jnp.float32)
        slot_values = slot_values + jnp.dot(
            lower_half, upper_rows, preferred_element_type=jnp.float32
        )
        return slot_values.astype(jnp.bfloat16).reshape(elem_count, side_count * trace_width)

    base_residual, base_stab = (
        lax.all_gather(trace_residual, "face", axis=0, tiled=True),
        lax.all_gather(stabilization, "face", axis=0, tiled=True),
    )
    local_part = jnp.einsum(
        "evk,ek->ev", vol_inverse, vol_residual, preferred_element_type=jnp.float32
    )
    trace_load = jnp.einsum(
        "etv,ev->et",
        trace_from_vol,
        local_part.astype(jnp.bfloat16),
        preferred_element_type=jnp.float32,
    )
    load_sums = assemble(trace_load.reshape(slot_count, trace_width))
    couple = jnp.einsum(
        "evk,ekt->evt", vol_inverse, vol_from_trace, preferred_element_type=jnp.float32
    ).astype(jnp.bfloat16)
    schur_block = jnp.einsum(
        "etv,evs->ets", trace_from_vol, couple, preferred_element_type=jnp.float32
    ).astype(jnp.bfloat16)
    right_side = base_residual - load_sums
    trace_now = right_side / base_stab
    for sweep_index in range(SWEEPS - 1):
        lam_elem = distribute(trace_now.astype(jnp.bfloat16))
        image_terms = jnp.einsum(
            "ets,es->et", schur_block, lam_elem, preferred_element_type=jnp.float32
        )
        image_sums = assemble(image_terms.reshape(slot_count, trace_width))
        trace_now = (right_side + image_sums) / base_stab
    lam_elem = distribute(trace_now.astype(jnp.bfloat16))
    vol_update = local_part - jnp.einsum(
        "evt,et->ev", couple, lam_elem, preferred_element_type=jnp.float32
    )
    trace_now = lax.dynamic_slice_in_dim(
        trace_now, lax.axis_index("face") * own_faces, own_faces, 0
    )
    return (trace_now, vol_update)


def solution(mesh):
    in_specs = (
        P(("elem", "face"), None, None),
        P(("elem", "face"), None, None),
        P(("elem", "face"), None, None),
        P(("elem", "face"), None),
        P(("elem", "face"), None),
        P(("elem", "face"), None),
        P(("elem", "face"), None),
    )
    out_specs = (P(("elem", "face"), None), P(("elem", "face"), None))
    return jax.shard_map(local, mesh=mesh, in_specs=in_specs, out_specs=out_specs, check_vma=False)
```

profile of v0, /device:TPU:1, one launch (start us, length us, event | category | flops | bytes accessed | tf_op | source)
XLA Modules:
  0.0 246.9 jit_solution(16300925224219799140)
XLA Ops:
  0.7 1.7 fusion.22
  2.5 0.3 fusion.20
  2.8 0.1 sub.41
  2.9 0.8 fusion.9
  3.8 18.0 %collective-permute-start = (f32[32,80]{0,1:T(8,128)}, f32[32,80]{0,1:T(8,128)}, u32[]{:S(2)}, u32[]{:S(2)}) collective-permute-start(f32[32,80]{0,1:T(8,128)} %fusion.9), channel_id=1, source_target_pairs={{8,0},{16,8},{24,16},{32,24},{40,32},{48,40},{56,48},{64,56},{72,6... | collective-permute-start | bytes 30728 | tf_op jit(solution)/shard_map/ppermute | solution.py:15
  21.9 0.2 fusion.19
  22.2 13.9 %all-gather.1 = f32[8,12,80]{2,1,0:T(8,128)S(1)} all-gather(f32[1,12,80]{2,1,0:T(8,128)S(1)} %bitcast.82), channel_id=1, replica_groups=mesh['elem'=96,'face'=8] {'face'}, dimensions={0}, use_global_device_ids=true | all-gather | bytes 34560 | tf_op jit(solution)/shard_map/all_gather | solution.py:66
  36.2 2.2 convolution_convert_fusion.1
  38.4 1.2 convolution_convert_fusion
  39.6 12.8 %all-gather = f32[8,12,80]{2,1,0:T(8,128)S(1)} all-gather(f32[1,12,80]{2,1,0:T(8,128)S(1)} %bitcast.83), channel_id=1, replica_groups=mesh['elem'=96,'face'=8] {'face'}, dimensions={0}, use_global_device_ids=true | all-gather | bytes 34560 | tf_op jit(solution)/shard_map/all_gather | solution.py:65
  52.5 0.8 slice_add_fusion.4
  53.4 22.8 %psum.35 = f32[96,80]{0,1:T(8,128)S(1)} all-reduce(f32[96,80]{0,1:T(8,128)S(1)} %pad_maximum_fusion), channel_id=1, replica_groups=mesh['elem'=96,'face'=8] {'face'}, use_global_device_ids=true, to_apply=%region_0.1 | all-reduce | flops 7680 | bytes 61440 | tf_op jit(solution)/shard_map/psum | solution.py:53
  76.2 1.9 collective-permute-start.1
  78.1 0.2 fusion.18
  78.3 5.7 %collective-permute-done.1 = bf16[32,80]{0,1:T(8,128)(2,1)S(1)} collective-permute-done((bf16[32,80]{0,1:T(8,128)(2,1)S(1)}, bf16[32,80]{0,1:T(8,128)(2,1)S(1)}, u32[]{:S(2)}, u32[]{:S(2)}) %collective-permute-start.1) | collective-permute-done | bytes 5152 | tf_op jit(solution)/shard_map/ppermute | solution.py:15
  84.1 0.2 fusion
  84.2 0.1 reshape.78
  84.3 0.4 fusion.46
  84.8 0.2 fusion.8
  85.0 1.9 collective-permute-start.2
  87.0 0.2 fusion.17
  87.3 2.5 %collective-permute-done.2 = f32[32,80]{0,1:T(8,128)S(1)} collective-permute-done((f32[32,80]{0,1:T(8,128)S(1)}, f32[32,80]{0,1:T(8,128)S(1)}, u32[]{:S(2)}, u32[]{:S(2)}) %collective-permute-start.2) | collective-permute-done | bytes 10272 | tf_op jit(solution)/shard_map/ppermute | solution.py:15
  89.9 26.6 %psum.36 = f32[96,80]{0,1:T(8,128)S(1)} all-reduce(f32[96,80]{0,1:T(8,128)S(1)} %pad_maximum_fusion.1), channel_id=1, replica_groups=mesh['elem'=96,'face'=8] {'face'}, use_global_device_ids=true, to_apply=%region_1.2 | all-reduce | flops 7680 | bytes 61440 | tf_op jit(solution)/shard_map/psum | solution.py:53
  116.5 1.9 collective-permute-start.3
  118.4 0.2 fusion.16
  118.6 5.7 %collective-permute-done.3 = bf16[32,80]{0,1:T(8,128)(2,1)S(1)} collective-permute-done((bf16[32,80]{0,1:T(8,128)(2,1)S(1)}, bf16[32,80]{0,1:T(8,128)(2,1)S(1)}, u32[]{:S(2)}, u32[]{:S(2)}) %collective-permute-start.3) | collective-permute-done | bytes 5152 | tf_op jit(solution)/shard_map/ppermute | solution.py:15
  124.3 0.2 fusion.1
  124.5 0.1 reshape.80
  124.6 0.4 fusion.47
  125.1 0.2 fusion.7
  125.3 1.9 collective-permute-start.4
  127.2 0.2 fusion.15
  127.6 2.5 %collective-permute-done.4 = f32[32,80]{0,1:T(8,128)S(1)} collective-permute-done((f32[32,80]{0,1:T(8,128)S(1)}, f32[32,80]{0,1:T(8,128)S(1)}, u32[]{:S(2)}, u32[]{:S(2)}) %collective-permute-start.4) | collective-permute-done | bytes 10272 | tf_op jit(solution)/shard_map/ppermute | solution.py:15
  130.2 26.2 %psum.37 = f32[96,80]{0,1:T(8,128)S(1)} all-reduce(f32[96,80]{0,1:T(8,128)S(1)} %pad_maximum_fusion.2), channel_id=1, replica_groups=mesh['elem'=96,'face'=8] {'face'}, use_global_device_ids=true, to_apply=%region_2.3 | all-reduce | flops 7680 | bytes 61440 | tf_op jit(solution)/shard_map/psum | solution.py:53
  156.4 1.9 collective-permute-start.5
  158.3 0.2 fusion.14
  158.5 5.7 %collective-permute-done.5 = bf16[32,80]{0,1:T(8,128)(2,1)S(1)} collective-permute-done((bf16[32,80]{0,1:T(8,128)(2,1)S(1)}, bf16[32,80]{0,1:T(8,128)(2,1)S(1)}, u32[]{:S(2)}, u32[]{:S(2)}) %collective-permute-start.5) | collective-permute-done | bytes 5152 | tf_op jit(solution)/shard_map/ppermute | solution.py:15
  164.2 0.2 fusion.2
  164.4 0.1 reshape.82
  164.5 0.4 fusion.48
  165.0 0.2 fusion.6
  165.2 1.9 collective-permute-start.6
  167.2 0.2 fusion.13
  167.5 2.5 %collective-permute-done.6 = f32[32,80]{0,1:T(8,128)S(1)} collective-permute-done((f32[32,80]{0,1:T(8,128)S(1)}, f32[32,80]{0,1:T(8,128)S(1)}, u32[]{:S(2)}, u32[]{:S(2)}) %collective-permute-start.6) | collective-permute-done | bytes 10272 | tf_op jit(solution)/shard_map/ppermute | solution.py:15
  170.1 26.2 %psum.38 = f32[96,80]{0,1:T(8,128)S(1)} all-reduce(f32[96,80]{0,1:T(8,128)S(1)} %pad_maximum_fusion.3), channel_id=1, replica_groups=mesh['elem'=96,'face'=8] {'face'}, use_global_device_ids=true, to_apply=%region_3.4 | all-reduce | flops 7680 | bytes 61440 | tf_op jit(solution)/shard_map/psum | solution.py:53
  196.3 1.9 collective-permute-start.7
  198.2 0.2 fusion.12
  198.4 5.7 %collective-permute-done.7 = bf16[32,80]{0,1:T(8,128)(2,1)S(1)} collective-permute-done((bf16[32,80]{0,1:T(8,128)(2,1)S(1)}, bf16[32,80]{0,1:T(8,128)(2,1)S(1)}, u32[]{:S(2)}, u32[]{:S(2)}) %collective-permute-start.7) | collective-permute-done | bytes 5152 | tf_op jit(solution)/shard_map/ppermute | solution.py:15
  204.2 0.2 fusion.3
  204.3 0.1 reshape.84
  204.4 0.4 fusion.49
  204.9 0.2 fusion.5
  205.1 1.9 collective-permute-start.8
  207.1 0.2 fusion.11
  207.4 2.5 %collective-permute-done.8 = f32[32,80]{0,1:T(8,128)S(1)} collective-permute-done((f32[32,80]{0,1:T(8,128)S(1)}, f32[32,80]{0,1:T(8,128)S(1)}, u32[]{:S(2)}, u32[]{:S(2)}) %collective-permute-start.8) | collective-permute-done | bytes 10272 | tf_op jit(solution)/shard_map/ppermute | solution.py:15
  210.0 26.2 %psum.39 = f32[96,80]{0,1:T(8,128)S(1)} all-reduce(f32[96,80]{0,1:T(8,128)S(1)} %pad_maximum_fusion.4), channel_id=1, replica_groups=mesh['elem'=96,'face'=8] {'face'}, use_global_device_ids=true, to_apply=%region_4.5 | all-reduce | flops 7680 | bytes 61440 | tf_op jit(solution)/shard_map/psum | solution.py:53
  236.2 0.2 fusion.10
  236.4 1.9 collective-permute-start.9
  238.4 0.7 copy.40
  239.1 5.2 %collective-permute-done.9 = bf16[32,80]{0,1:T(8,128)(2,1)S(1)} collective-permute-done((bf16[32,80]{0,1:T(8,128)(2,1)S(1)}, bf16[32,80]{0,1:T(8,128)(2,1)S(1)}, u32[]{:S(2)}, u32[]{:S(2)}) %collective-permute-start.9) | collective-permute-done | bytes 5152 | tf_op jit(solution)/shard_map/ppermute | solution.py:15
  244.2 0.2 fusion.4
  244.4 0.1 reshape.86
  244.5 1.8 fusion.50
  246.3 0.6 bitcast_subtract_fusion
  (54 shorter events, 1.7 us)
Async XLA Ops:
  0.6 1.8 copy-start
  0.6 2.2 copy-start.7
  0.7 21.5 %copy-start.5 = (f32[12,80]{1,0:T(8,128)S(1)}, f32[12,80]{1,0:T(8,128)}, u32[]{:S(2)}) copy-start(f32[12,80]{1,0:T(8,128)} %param.13) | copy-start | bytes 11524
  0.7 35.5 %copy-start.2 = (bf16[4,320,320]{2,1,0:T(8,128)(2,1)S(1)}, bf16[4,320,320]{2,1,0:T(8,128)(2,1)}, u32[]{:S(2)}) copy-start(bf16[4,320,320]{2,1,0:T(8,128)(2,1)} %param.7) | copy-start | bytes 2457604
  2.4 33.7 %copy-start.3 = (f32[4,1,320]{2,1,0:T(1,128)}, f32[4,1,320]{2,1,0:T(1,128)S(1)}, u32[]{:S(2)}) copy-start(f32[4,1,320]{2,1,0:T(1,128)S(1)} %fusion.22) | copy-start | bytes 15364
  3.8 48.7 %collective-permute-start = (f32[32,80]{0,1:T(8,128)}, f32[32,80]{0,1:T(8,128)}, u32[]{:S(2)}, u32[]{:S(2)}) collective-permute-start(f32[32,80]{0,1:T(8,128)} %fusion.9), channel_id=1, source_target_pairs={{8,0},{16,8},{24,16},{32,24},{40,32},{48,40},{56,48},{64,56},{72,6... | collective-permute-start | bytes 30728 | tf_op jit(solution)/shard_map/ppermute | solution.py:15
  38.4 1.3 copy-start.1
  38.4 1.3 copy-start.6
  76.2 7.8 %collective-permute-start.1 = (bf16[32,80]{0,1:T(8,128)(2,1)S(1)}, bf16[32,80]{0,1:T(8,128)(2,1)S(1)}, u32[]{:S(2)}, u32[]{:S(2)}) collective-permute-start(bf16[32,80]{0,1:T(8,128)(2,1)S(1)} %bitcast.80), channel_id=1, source_target_pairs={{760,0},{0,8},{8,16},{16,24},{24,32},{32,40},{40,48},{48,56},{56,6... | collective-permute-start | bytes 15368 | tf_op jit(solution)/shard_map/ppermute | solution.py:15
  85.0 4.7 %collective-permute-start.2 = (f32[32,80]{0,1:T(8,128)S(1)}, f32[32,80]{0,1:T(8,128)S(1)}, u32[]{:S(2)}, u32[]{:S(2)}) collective-permute-start(f32[32,80]{0,1:T(8,128)S(1)} %fusion.8), channel_id=1, source_target_pairs={{8,0},{16,8},{24,16},{32,24},{40,32},{48,40},{56,48},{64,56},{72,6... | collective-permute-start | bytes 30728 | tf_op jit(solution)/shard_map/ppermute | solution.py:15
  116.5 7.8 %collective-permute-start.3 = (bf16[32,80]{0,1:T(8,128)(2,1)S(1)}, bf16[32,80]{0,1:T(8,128)(2,1)S(1)}, u32[]{:S(2)}, u32[]{:S(2)}) collective-permute-start(bf16[32,80]{0,1:T(8,128)(2,1)S(1)} %bitcast.76), channel_id=1, source_target_pairs={{760,0},{0,8},{8,16},{16,24},{24,32},{32,40},{40,48},{48,56},{56,6... | collective-permute-start | bytes 15368 | tf_op jit(solution)/shard_map/ppermute | solution.py:15
  125.3 4.7 %collective-permute-start.4 = (f32[32,80]{0,1:T(8,128)S(1)}, f32[32,80]{0,1:T(8,128)S(1)}, u32[]{:S(2)}, u32[]{:S(2)}) collective-permute-start(f32[32,80]{0,1:T(8,128)S(1)} %fusion.7), channel_id=1, source_target_pairs={{8,0},{16,8},{24,16},{32,24},{40,32},{48,40},{56,48},{64,56},{72,6... | collective-permute-start | bytes 30728 | tf_op jit(solution)/shard_map/ppermute | solution.py:15
  156.4 7.8 %collective-permute-start.5 = (bf16[32,80]{0,1:T(8,128)(2,1)S(1)}, bf16[32,80]{0,1:T(8,128)(2,1)S(1)}, u32[]{:S(2)}, u32[]{:S(2)}) collective-permute-start(bf16[32,80]{0,1:T(8,128)(2,1)S(1)} %bitcast.77), channel_id=1, source_target_pairs={{760,0},{0,8},{8,16},{16,24},{24,32},{32,40},{40,48},{48,56},{56,6... | collective-permute-start | bytes 15368 | tf_op jit(solution)/shard_map/ppermute | solution.py:15
  165.2 4.7 %collective-permute-start.6 = (f32[32,80]{0,1:T(8,128)S(1)}, f32[32,80]{0,1:T(8,128)S(1)}, u32[]{:S(2)}, u32[]{:S(2)}) collective-permute-start(f32[32,80]{0,1:T(8,128)S(1)} %fusion.6), channel_id=1, source_target_pairs={{8,0},{16,8},{24,16},{32,24},{40,32},{48,40},{56,48},{64,56},{72,6... | collective-permute-start | bytes 30728 | tf_op jit(solution)/shard_map/ppermute | solution.py:15
  196.3 7.8 %collective-permute-start.7 = (bf16[32,80]{0,1:T(8,128)(2,1)S(1)}, bf16[32,80]{0,1:T(8,128)(2,1)S(1)}, u32[]{:S(2)}, u32[]{:S(2)}) collective-permute-start(bf16[32,80]{0,1:T(8,128)(2,1)S(1)} %bitcast.78), channel_id=1, source_target_pairs={{760,0},{0,8},{8,16},{16,24},{24,32},{32,40},{40,48},{48,56},{56,6... | collective-permute-start | bytes 15368 | tf_op jit(solution)/shard_map/ppermute | solution.py:15
  204.8 41.5 %copy-start.4 = (f32[4,1,320]{2,1,0:T(1,128)S(1)}, f32[4,1,320]{2,1,0:T(1,128)}, u32[]{:S(2)}) copy-start(f32[4,1,320]{2,1,0:T(1,128)} %copy-done.3) | copy-start | bytes 15364
  205.1 4.7 %collective-permute-start.8 = (f32[32,80]{0,1:T(8,128)S(1)}, f32[32,80]{0,1:T(8,128)S(1)}, u32[]{:S(2)}, u32[]{:S(2)}) collective-permute-start(f32[32,80]{0,1:T(8,128)S(1)} %fusion.5), channel_id=1, source_target_pairs={{8,0},{16,8},{24,16},{32,24},{40,32},{48,40},{56,48},{64,56},{72,6... | collective-permute-start | bytes 30728 | tf_op jit(solution)/shard_map/ppermute | solution.py:15
  236.4 7.8 %collective-permute-start.9 = (bf16[32,80]{0,1:T(8,128)(2,1)S(1)}, bf16[32,80]{0,1:T(8,128)(2,1)S(1)}, u32[]{:S(2)}, u32[]{:S(2)}) collective-permute-start(bf16[32,80]{0,1:T(8,128)(2,1)S(1)} %bitcast.79), channel_id=1, source_target_pairs={{760,0},{0,8},{8,16},{16,24},{24,32},{32,40},{40,48},{48,56},{56,6... | collective-permute-start | bytes 15368 | tf_op jit(solution)/shard_map/ppermute | solution.py:15
where the time goes:
time: 248 us; the launch traced here: 247 us
  blocking collectives  155 us (62%)
  waiting for transfers between devices  38.2 us (15%)
  starting transfers between devices  35.3 us (14%)
  matrix products  13.3 us (5%)
    psum x5, blocking collectives, assemble(): summed = lax.psum(partial_value, 'face')  128 us
    ppermute x10, waiting for transfers between devices, shifted(): return lax.ppermute(block, axis, route)  38.2 us
    ppermute x10, starting transfers between devices, shifted(): return lax.ppermute(block, axis, route)  35.3 us
    all_gather x1, blocking collectives, local(): lax.all_gather(stabilization, 'face', axis=0, tiled=True)  13.9 us
    all_gather x1, blocking collectives, local(): lax.all_gather(trace_residual, 'face', axis=0, tiled=True)  12.8 us
  transfers between devices with their start and end apart: 10, of which 9 were waited for; matrix products, arithmetic and copies ran while one was open for 3% of the time, Pallas kernels for 0%

commit v1 on v0

v1 whole, which is shorter than its diff:
```python
import functools

import jax
import jax.numpy as jnp
from jax import lax
from jax.experimental import pallas as pl
from jax.experimental.pallas import tpu as pltpu
from jax.sharding import PartitionSpec as P

MESH = pl.DeviceIdType.MESH
F32, BF16, I32 = jnp.float32, jnp.bfloat16, jnp.int32
SWEEPS = 5
ROWS, PARTS, SLOTS, OWN = 16, 5, 24, 12
TURNS = (4, 3, 5, 2, 6, 1, 7)
PEERS = tuple((1, i) for i in TURNS + (0,)) + tuple((-1, i) for i in TURNS + (0,)) + tuple((0, i) for i in TURNS)
SELF = len(PEERS)
KINDS = SELF + 1


def kernel(groups, members, ids, inv_hbm, up_hbm, down_hbm, vol_res, res_ref, stab_ref, trace_out, vol_out,
           inv, up, down, couple, schur, rhs_mat, first, tiles, pick, face_pick, kind_row, square,
           load_sem, send_sem, recv_sem):
    group, member = lax.axis_index("elem"), lax.axis_index("face")
    group_faces = OWN * members

    def device(shift, turn):
        return (lax.rem(group + shift + groups, groups), lax.rem(member + turn + members, members))

    loads = [
        pltpu.make_async_copy(src, dst, load_sem.at[n])
        for n, (src, dst) in enumerate(((inv_hbm, inv), (down_hbm, down), (up_hbm, up)))
    ]
    for copy in loads:
        copy.start()
    barrier = pltpu.get_barrier_semaphore()
    for shift, turn in PEERS:
        pl.semaphore_signal(barrier, inc=1, device_id=device(shift, turn), device_id_type=MESH)

    lane = lax.broadcasted_iota(I32, (1, 256), 1)

    def steps(x, width, count):
        return sum((x >= width * n).astype(I32) for n in range(1, count))

    half = lane >= 128
    inner = jnp.where(half, lax.bitwise_and(lane, 63), lane)
    part = jnp.where(half, steps(inner, OWN, PARTS), steps(inner, SLOTS, PARTS))
    index = inner - part * jnp.where(half, OWN, SLOTS)
    used = inner < jnp.where(half, OWN * PARTS, SLOTS * PARTS)
    own_base = group * group_faces + member * OWN
    wanted = own_base + index
    for s in range(SLOTS):
        wanted = jnp.where(jnp.logical_and(lane < 128, index == s), ids[s % 4, s // 4], wanted)
    wanted = jnp.where(used, wanted, -1)
    wanted_f = wanted.astype(F32)

    square[...] = jnp.zeros_like(square)
    square[0:OWN, 0:80] = res_ref[...]
    square[64 : 64 + OWN, 0:80] = stab_ref[...]
    turned = square[...].T
    small = lax.broadcasted_iota(I32, (ROWS, 128), 1)
    low = lax.bitwise_and(small, 63)
    faces = jnp.zeros((ROWS, 128), F32)
    for j in range(PARTS):
        block = turned[j * ROWS : (j + 1) * ROWS]
        block = pltpu.roll(block, j * OWN, 1) if j else block
        faces = jnp.where(jnp.logical_and(low >= j * OWN, low < (j + 1) * OWN), block, faces)
    first[SELF, 0:ROWS] = faces
    first[SELF, ROWS : ROWS + 8] = jnp.broadcast_to(wanted_f[:, :128], (8, 128))

    def send(phase, ref):
        for n, (shift, turn) in enumerate(PEERS):
            pltpu.make_async_remote_copy(
                src_ref=ref.at[SELF],
                dst_ref=ref.at[n],
                send_sem=send_sem.at[phase],
                recv_sem=recv_sem.at[phase],
                device_id=device(shift, turn),
                device_id_type=MESH,
            ).start()

    def arrive(phase, ref, sem):
        some = ref.at[pl.ds(0, SELF)]
        pltpu.make_async_copy(some, some, sem.at[phase]).wait()

    pl.semaphore_wait(barrier, SELF)
    send(0, first)

    def merged(products):
        total = products[0]
        for e in range(1, 4):
            at = lax.broadcasted_iota(I32, total.shape, 1)
            total = jnp.where(at == e, products[e], total)
        return total

    def to_tile(column):
        tile = jnp.zeros((ROWS, 128), F32)
        for j in range(PARTS):
            for k in range(6):
                begin = k * 80 + j * ROWS
                place = j * SLOTS + k * 4
                block = column[begin : begin + ROWS]
                block = pltpu.roll(block, place, 1) if place else block
                tile = jnp.where(jnp.logical_and(small >= place, small < place + 4), block, tile)
        return tile

    loads[0].wait()
    res_rows = jnp.concatenate([vol_res[...], jnp.zeros((124, 320), BF16)], axis=0)
    across = (((1,), (1,)), ((), ()))
    local = merged([
        lax.dot_general(inv[e], res_rows, across, preferred_element_type=F32) for e in range(4)
    ])
    local_half = local.astype(BF16)
    loads[1].wait()
    own = to_tile(merged([jnp.dot(down[e], local_half, preferred_element_type=F32) for e in range(4)]))
    tiles[0, SELF] = own.astype(BF16)
    send(1, tiles.at[0])

    loads[2].wait()
    rhs_mat[480:512] = jnp.zeros((32, 128), BF16)

    def condense(e, carry):
        block = jnp.dot(inv[e], up[e], preferred_element_type=F32).astype(BF16)
        block = jnp.concatenate([block, jnp.zeros((320, 32), BF16)], axis=1)
        couple[e] = block
        schur[e] = jnp.dot(down[e], block, preferred_element_type=F32).astype(BF16)
        return carry

    lax.fori_loop(0, 4, condense, 0)

    arrive(0, first, recv_sem)
    eight = lax.broadcasted_iota(I32, (8, 128), 0)
    for base in range(0, KINDS, 8):
        rows = jnp.zeros((8, 128), F32)
        for n in range(8):
            rows = jnp.where(eight == n, first[base + n, ROWS : ROWS + 8], rows)
        square[base : base + 8] = rows
    square[KINDS:32] = jnp.zeros((32 - KINDS, 128), F32)
    held = square[...].T
    slot_row = lax.broadcasted_iota(I32, (SLOTS, 256), 0)
    wide = jnp.broadcast_to(wanted_f, (SLOTS, 256))
    total = jnp.zeros((SLOTS, 256), F32)
    least = jnp.full((SLOTS, 256), 4096.0, F32)
    for n in range(KINDS):
        hit = jnp.broadcast_to(held[0:SLOTS, n : n + 1], (SLOTS, 256)) == wide
        code = (slot_row + 32 * n).astype(F32)
        total = total + jnp.where(hit, code, 0.0)
        least = jnp.minimum(least, jnp.where(hit, code, 4096.0))
    total = jnp.sum(total, axis=0, keepdims=True)
    least = jnp.min(least, axis=0, keepdims=True)
    self_code = (SELF * 32 + index).astype(F32)
    code = jnp.where(half, jnp.where(lane < 192, least, total - least), total - self_code)
    code = code.astype(I32)
    kinds = jnp.where(used, lax.shift_right_arithmetic(code, 5), -1)
    row = part * SLOTS + lax.bitwise_and(code, 31)
    deep = lax.broadcasted_iota(I32, (128, 256), 0)
    pick[...] = jnp.where(jnp.logical_and(deep == row, used), 1.0, 0.0).astype(BF16)
    kind_row[...] = jnp.broadcast_to(kinds, (ROWS, 256))

    owner = jnp.full((1, 128), -1, I32)
    place = jnp.zeros((1, 128), I32)
    sources = [n for n in range(SELF) if PEERS[n][0] >= 0] + [SELF]
    for n in sources:
        shift, turn = PEERS[n] if n < SELF else (0, 0)
        base = lax.rem(group - shift + groups, groups) * group_faces + lax.rem(member - turn + members, members) * OWN
        offset = wanted[:, :128] - base
        hit = jnp.logical_and(offset >= 0, offset < OWN)
        owner = jnp.where(hit, n, owner)
        place = jnp.where(hit, offset, place)
    place = part[:, :128] * OWN + place
    slim = lax.broadcasted_iota(I32, (128, 128), 0)
    face_pick[:, 0:128] = jnp.where(slim == place, 1.0, 0.0)
    face_pick[:, 128:256] = jnp.where(slim == place + 64, 1.0, 0.0)
    sent = jnp.concatenate([first[n, 0:ROWS] for n in sources], axis=0)
    found = jnp.dot(sent, face_pick[...], preferred_element_type=F32, precision=lax.Precision.HIGHEST)
    owner_rows = jnp.broadcast_to(owner, (ROWS, 128))
    right = jnp.zeros((ROWS, 128), F32)
    stab = jnp.zeros((ROWS, 128), F32)
    for at, n in enumerate(sources):
        block = found[at * ROWS : (at + 1) * ROWS]
        right = jnp.where(owner_rows == n, block[:, :128], right)
        stab = jnp.where(owner_rows == n, block[:, 128:], stab)
    scale = 1.0 / jnp.where(owner_rows >= 0, stab, 1.0)
    face_stab = pltpu.roll(first[SELF, 0:ROWS], 64, 1)
    face_scale = 1.0 / jnp.where(small < OWN * PARTS, face_stab, 1.0)

    def gathered(phase, width):
        stack = tiles[phase].reshape(KINDS * ROWS, 128)
        found = jnp.dot(stack, pick[:, 0:width], preferred_element_type=F32)
        kinds = kind_row[:, 0:width]
        total = jnp.zeros((ROWS, width), F32)
        for n in range(KINDS):
            total = jnp.where(kinds == n, found[n * ROWS : (n + 1) * ROWS], total)
        return total

    def face_sum(both):
        return both[:, 128:] + pltpu.roll(both[:, 128:], 64, 1)

    def spread(lam):
        for k in range(6):
            for j in range(PARTS):
                place = j * SLOTS + k * 4
                block = pltpu.roll(lam, 128 - place, 1) if place else lam
                rhs_mat[k * 80 + j * ROWS : k * 80 + (j + 1) * ROWS] = block.astype(BF16)

    arrive(1, tiles.at[0], recv_sem)
    both = gathered(0, 256)
    right = right - (own + both[:, :128])
    face_right = first[SELF, 0:ROWS] - face_sum(both)
    spread(right * scale)
    for sweep in range(1, SWEEPS):
        own = to_tile(merged([
            jnp.dot(schur[e], rhs_mat[...], preferred_element_type=F32) for e in range(4)
        ]))
        tiles[sweep, SELF] = own.astype(BF16)
        send(sweep + 1, tiles.at[sweep])
        arrive(sweep + 1, tiles.at[sweep], recv_sem)
        both = gathered(sweep, 256 if sweep == SWEEPS - 1 else 128)
        spread((right + own + both[:, :128]) * scale)

    face_now = (face_right + face_sum(both)) * face_scale
    for j in range(PARTS):
        block = pltpu.roll(face_now, 128 - j * OWN, 1) if j else face_now
        square[j * ROWS : (j + 1) * ROWS] = block
    trace_out[...] = square[...].T[0:OWN, 0:80]
    back = merged([jnp.dot(couple[e], rhs_mat[...], preferred_element_type=F32) for e in range(4)])
    answer = jnp.concatenate([local - back, jnp.zeros((64, 128), F32)], axis=0)
    for n in range(3):
        width = min(128, 320 - n * 128)
        vol_out[:, n * 128 : n * 128 + width] = answer[n * 128 : (n + 1) * 128].T[0:4, 0:width]

    arrive(0, first, send_sem)
    for phase in range(SWEEPS):
        arrive(phase + 1, tiles.at[phase], send_sem)


def solution(mesh):
    groups, members = mesh.shape["elem"], mesh.shape["face"]
    spec2, spec3 = P(("elem", "face"), None), P(("elem", "face"), None, None)

    def local(vol_inverse, vol_from_trace, trace_from_vol, vol_residual, face_ids, trace_residual, stabilization):
        vmem, hbm = pl.BlockSpec(memory_space=pltpu.VMEM), pl.BlockSpec(memory_space=pl.ANY)
        return pl.pallas_call(
            functools.partial(kernel, groups, members),
            out_shape=(
                jax.ShapeDtypeStruct(trace_residual.shape, F32),
                jax.ShapeDtypeStruct(vol_residual.shape, F32),
            ),
            in_specs=[pl.BlockSpec(memory_space=pltpu.SMEM), hbm, hbm, hbm, vmem, vmem, vmem],
            out_specs=(vmem, vmem),
            scratch_shapes=[
                pltpu.VMEM((4, 320, 320), BF16),
                pltpu.VMEM((4, 320, 480), BF16),
                pltpu.VMEM((4, 480, 320), BF16),
                pltpu.VMEM((4, 320, 512), BF16),
                pltpu.VMEM((4, 480, 512), BF16),
                pltpu.VMEM((512, 128), BF16),
                pltpu.VMEM((KINDS, ROWS + 8, 128), F32),
                pltpu.VMEM((SWEEPS, KINDS, ROWS, 128), BF16),
                pltpu.VMEM((128, 256), BF16),
                pltpu.VMEM((128, 256), F32),
                pltpu.VMEM((ROWS, 256), I32),
                pltpu.VMEM((128, 128), F32),
                pltpu.SemaphoreType.DMA((3,)),
                pltpu.SemaphoreType.DMA((SWEEPS + 1,)),
                pltpu.SemaphoreType.DMA((SWEEPS + 1,)),
            ],
            compiler_params=pltpu.CompilerParams(collective_id=0, has_side_effects=True),
            name="newton",
        )(face_ids, vol_inverse, vol_from_trace, trace_from_vol, vol_residual, trace_residual, stabilization)

    return jax.shard_map(
        local,
        mesh=mesh,
        in_specs=(spec3, spec3, spec3, spec2, spec2, spec2, spec2),
        out_specs=(spec2, spec2),
        check_vma=False,
    )
```

time: 248 us -> 59.9 us (0.24)
  blocking collectives: 155 us -> 0 us
  Pallas kernels: 0 us -> 53.9 us
  waiting for transfers between devices: 38.2 us -> 0 us
  starting transfers between devices: 35.3 us -> 0 us
  matrix products: 13.3 us -> 0 us
  local copies, waits for them, and re-layouts: 2.39 us -> 5.12 us
    psum x5 -> x0, blocking collectives: 128 us -> none  [assemble(): summed = lax.psum(partial_value, 'face')]
    pallas_call x0 -> x1, Pallas kernels: none -> 53.9 us  [local(): pl.pallas_call(functools.partial(kernel, groups, members), out_shape=(jax...]
    ppermute x10 -> x0, waiting for transfers between devices: 38.2 us -> none  [shifted(): return lax.ppermute(block, axis, route)]
    ppermute x10 -> x0, starting transfers between devices: 35.3 us -> none  [shifted(): return lax.ppermute(block, axis, route)]
    all_gather x2 -> x0, blocking collectives: 26.6 us -> none  [the longest x1 13.9 us: local(): lax.all_gather(stabilization, 'face', axis=0, tiled=True)]
    dot_general x29 -> x0, matrix products: 13.3 us -> none  [the longest x1 2.16 us: local(): jnp.einsum('evk,ekt->evt', vol_inverse, vol_from_trace, preferred_element...]
    unnamed x21 -> x3, local copies, waits for them, and re-layouts: 0.88 us -> 5.12 us
  transfers between devices with their start and end apart: 10 -> 0, of which waited for: 9 -> 0; matrix products, arithmetic and copies ran while one was open for 3% -> 0% of each run, Pallas kernels for 0% -> 0%
where the time goes in v1:
time: 59.9 us; the launch traced here: 59.7 us
  Pallas kernels  53.9 us (90%)
  local copies, waits for them, and re-layouts  5.12 us (9%)
  between operations  0.64 us (1%)
    pallas_call x1, Pallas kernels, local(): pl.pallas_call(functools.partial(kernel, groups, members), out_shape=(jax...  53.9 us
    unnamed x3, local copies, waits for them, and re-layouts  5.12 us

profile of v1, /device:TPU:1, one launch (start us, length us, event | category | flops | bytes accessed | tf_op | source)
XLA Modules:
  0.0 59.7 jit_solution(11023642655850443394)
XLA Ops:
  0.6 2.5 %copy.9.down_hbm = bf16[4,480,320]{2,1,0:T(8,128)(2,1)} copy(bf16[4,480,320]{1,2,0:T(8,128)(2,1)} %param.9) | data formatting | bytes 2457600 | tf_op args[2]
  3.2 53.9 %newton.1 = (f32[12,80]{1,0:T(8,128)}, f32[4,320]{1,0:T(4,128)}) custom-call(s32[4,6]{1,0:T(4,128)} %ids.1, bf16[4,320,320]{2,1,0:T(8,128)(2,1)} %inv_hbm.1, bf16[4,320,480]{2,1,0:T(8,128)(2,1)} %up_hbm.1, bf16[4,480,320]{2,1,0:T(8,128)(2,1)} %copy.9.down_hbm, bf16[4,320]{1,0:T(4,128)(2,1)} %vol_res.1, f32[12,80]{1,0:T(8,128)} %res_ref.1, f32[12,80]{1,0:T(8,128)} %stab_ref.1), custom_call_target="tpu_custom_call" | custom-call | tf_op jit(solution)/shard_map/newton/pallas_call | solution.py:242
  57.1 1.3 %copy.12 = f32[12,80]{1,0:T(8,128)} copy(f32[12,80]{1,0:T(8,128)} %get-tuple-element.4) | data formatting | bytes 7680
  58.4 1.3 %copy.13 = f32[4,320]{1,0:T(4,128)} copy(f32[4,320]{1,0:T(4,128)} %get-tuple-element.5) | data formatting | bytes 10240

commit v2 on v1

v2 whole, which is shorter than its diff:
```python
import functools

import jax
import jax.numpy as jnp
from jax import lax
from jax.experimental import pallas as pl
from jax.experimental.pallas import tpu as pltpu
from jax.sharding import PartitionSpec as P

MESH = pl.DeviceIdType.MESH
F32, BF16, I32 = jnp.float32, jnp.bfloat16, jnp.int32
SWEEPS = 5
ROWS, PARTS, SLOTS, OWN = 16, 5, 24, 12
TURNS = (4, 3, 5, 2, 6, 1, 7)
PEERS = tuple((1, i) for i in TURNS + (0,)) + tuple((-1, i) for i in TURNS + (0,)) + tuple((0, i) for i in TURNS)
SELF = len(PEERS)
KINDS = SELF + 1


def kernel(groups, members, ids_hbm, inv_hbm, up_hbm, down_hbm, vol_hbm, res_hbm, stab_hbm, trace_out, vol_out,
           ids, vol_res, res_ref, stab_ref, inv, up, down, couple, schur, rhs_mat, first, tiles, pick, face_pick,
           kind_row, square, load_sem, send_sem, recv_sem):
    group, member = lax.axis_index("elem"), lax.axis_index("face")
    group_faces = OWN * members

    def device(shift, turn):
        return (lax.rem(group + shift + groups, groups), lax.rem(member + turn + members, members))

    barrier = pltpu.get_barrier_semaphore()
    for shift, turn in PEERS:
        pl.semaphore_signal(barrier, inc=1, device_id=device(shift, turn), device_id_type=MESH)
    pairs = ((vol_hbm, vol_res), (inv_hbm, inv), (down_hbm, down), (ids_hbm, ids), (res_hbm, res_ref),
             (stab_hbm, stab_ref), (up_hbm, up))
    loads = [pltpu.make_async_copy(src, dst, load_sem.at[n]) for n, (src, dst) in enumerate(pairs)]
    for copy in loads:
        copy.start()

    lane = lax.broadcasted_iota(I32, (1, 256), 1)

    def steps(x, width, count):
        return sum((x >= width * n).astype(I32) for n in range(1, count))

    half = lane >= 128
    inner = jnp.where(half, lax.bitwise_and(lane, 63), lane)
    part = jnp.where(half, steps(inner, OWN, PARTS), steps(inner, SLOTS, PARTS))
    index = inner - part * jnp.where(half, OWN, SLOTS)
    used = inner < jnp.where(half, OWN * PARTS, SLOTS * PARTS)
    small = lax.broadcasted_iota(I32, (ROWS, 128), 1)
    low = lax.bitwise_and(small, 63)
    fourth = lax.bitwise_and(small, 3)
    for e in range(4):
        rhs_mat[e * 512 + 480 : (e + 1) * 512] = jnp.zeros((32, 128), BF16)

    def send(phase, ref):
        for n, (shift, turn) in enumerate(PEERS):
            pltpu.make_async_remote_copy(
                src_ref=ref.at[SELF],
                dst_ref=ref.at[n],
                send_sem=send_sem.at[phase],
                recv_sem=recv_sem.at[phase],
                device_id=device(shift, turn),
                device_id_type=MESH,
            ).start()

    def arrive(phase, ref, sem):
        some = ref.at[pl.ds(0, SELF)]
        pltpu.make_async_copy(some, some, sem.at[phase]).wait()

    loads[3].wait()
    own_base = group * group_faces + member * OWN
    wanted = own_base + index
    for s in range(SLOTS):
        wanted = jnp.where(jnp.logical_and(lane < 128, index == s), ids[s % 4, s // 4], wanted)
    wanted = jnp.where(used, wanted, -1)
    wanted_f = wanted.astype(F32)
    square[...] = jnp.zeros_like(square)
    loads[4].wait()
    square[0:OWN, 0:80] = res_ref[...]
    loads[5].wait()
    square[64 : 64 + OWN, 0:80] = stab_ref[...]
    turned = square[...].T
    faces = jnp.zeros((ROWS, 128), F32)
    for j in range(PARTS):
        block = turned[j * ROWS : (j + 1) * ROWS]
        block = pltpu.roll(block, j * OWN, 1) if j else block
        faces = jnp.where(jnp.logical_and(low >= j * OWN, low < (j + 1) * OWN), block, faces)
    first[SELF, 0:ROWS] = faces
    first[SELF, ROWS : ROWS + 8] = jnp.broadcast_to(wanted_f[:, :128], (8, 128))

    loads[0].wait()
    res_rows = jnp.concatenate([vol_res[...], jnp.zeros((124, 320), BF16)], axis=0)
    across = (((1,), (1,)), ((), ()))
    loads[1].wait()
    local = lax.dot_general(inv[0], res_rows, across, preferred_element_type=F32)
    at = lax.broadcasted_iota(I32, local.shape, 1)
    for e in range(1, 4):
        local = jnp.where(at == e, lax.dot_general(inv[e], res_rows, across, preferred_element_type=F32), local)
    local = jnp.concatenate([local, jnp.zeros((64, 128), F32)], axis=0)
    local = jnp.concatenate([local[n * 128 : (n + 1) * 128].T[0:ROWS] for n in range(3)], axis=1)
    local_rows = local[0:8]
    level = lax.broadcasted_iota(I32, (ROWS, 320), 0)
    local = jnp.concatenate(
        [jnp.where(level == e, local[:, 0:320], 0.0).astype(BF16) for e in range(4)], axis=1
    )
    loads[2].wait()
    load = jnp.zeros((ROWS, 480), F32)
    for e in range(4):
        load = load + jnp.dot(local[:, e * 320 : (e + 1) * 320], down[e], preferred_element_type=F32)
    load = jnp.concatenate([load, jnp.zeros((ROWS, 32), F32)], axis=1)
    load = jnp.concatenate([load, jnp.zeros((112, 512), F32)], axis=0)
    load = jnp.concatenate([load[:, n * 128 : (n + 1) * 128].T for n in range(4)], axis=0)
    own = jnp.zeros((ROWS, 128), F32)
    for j in range(PARTS):
        for k in range(6):
            begin = k * 80 + j * ROWS
            place = j * SLOTS + k * 4
            block = load[begin : begin + ROWS]
            block = pltpu.roll(block, place, 1) if place else block
            own = jnp.where(jnp.logical_and(small >= place, small < place + 4), block, own)
    tiles[0, SELF] = own.astype(BF16)

    pl.semaphore_wait(barrier, SELF)
    send(0, first)
    send(1, tiles.at[0])

    loads[6].wait()

    def condense(e, carry):
        block = jnp.dot(inv[e], up[e], preferred_element_type=F32).astype(BF16)
        block = jnp.concatenate([block, jnp.zeros((320, 32), BF16)], axis=1)
        columns = pl.ds(pl.multiple_of(e * 512, 512), 512)
        couple[:, columns] = block
        schur[:, columns] = lax.dot_general(
            down[e], block, (((0,), (0,)), ((), ())), preferred_element_type=F32
        ).astype(BF16)
        return carry

    lax.fori_loop(0, 4, condense, 0)

    arrive(0, first, recv_sem)
    eight = lax.broadcasted_iota(I32, (8, 128), 0)
    for base in range(0, KINDS, 8):
        rows = jnp.zeros((8, 128), F32)
        for n in range(8):
            rows = jnp.where(eight == n, first[base + n, ROWS : ROWS + 8], rows)
        square[base : base + 8] = rows
    square[KINDS:32] = jnp.zeros((32 - KINDS, 128), F32)
    held = square[...].T
    slot_row = lax.broadcasted_iota(I32, (SLOTS, 128), 0).astype(F32)
    wide_slot = jnp.broadcast_to(wanted_f[:, :128], (SLOTS, 128))
    wide_face = jnp.broadcast_to(wanted_f[:, 128:], (SLOTS, 128))
    slot_sum = jnp.zeros((SLOTS, 128), F32)
    face_total = jnp.zeros((SLOTS, 128), F32)
    least = jnp.full((SLOTS, 128), 4096.0, F32)
    for n in range(KINDS):
        column = jnp.broadcast_to(held[0:SLOTS, n : n + 1], (SLOTS, 128))
        code = slot_row + 32.0 * n
        slot_sum = slot_sum + jnp.where(column == wide_slot, code, 0.0)
        if n < SELF and PEERS[n][0] > 0:
            continue
        hit = column == wide_face
        face_total = face_total + jnp.where(hit, code, 0.0)
        least = jnp.minimum(least, jnp.where(hit, code, 4096.0))
    slot_sum = jnp.sum(slot_sum, axis=0, keepdims=True) - (SELF * 32 + index[:, :128]).astype(F32)
    face_total = jnp.sum(face_total, axis=0, keepdims=True)
    least = jnp.min(least, axis=0, keepdims=True)
    face_code = jnp.where(lane[:, :128] < 64, least, face_total - least)
    code = jnp.concatenate([slot_sum, face_code], axis=1).astype(I32)
    kinds = jnp.where(used, lax.shift_right_arithmetic(code, 5), -1)
    row = jnp.where(used, part * SLOTS + lax.bitwise_and(code, 31), -1)
    deep = lax.broadcasted_iota(I32, (128, 256), 0)
    pick[...] = jnp.where(deep == row, 1.0, 0.0).astype(BF16)
    kind_row[...] = jnp.broadcast_to(kinds, (ROWS, 256))

    owner = jnp.full((1, 128), -1, I32)
    place = jnp.zeros((1, 128), I32)
    sources = [n for n in range(SELF) if PEERS[n][0] >= 0] + [SELF]
    for n in sources:
        shift, turn = PEERS[n] if n < SELF else (0, 0)
        base = lax.rem(group - shift + groups, groups) * group_faces + lax.rem(member - turn + members, members) * OWN
        offset = wanted[:, :128] - base
        hit = jnp.logical_and(offset >= 0, offset < OWN)
        owner = jnp.where(hit, n, owner)
        place = jnp.where(hit, offset, place)
    place = part[:, :128] * OWN + place
    slim = lax.broadcasted_iota(I32, (128, 128), 0)
    face_pick[:, 0:128] = jnp.where(slim == place, 1.0, 0.0)
    face_pick[:, 128:256] = jnp.where(slim == place + 64, 1.0, 0.0)
    sent = jnp.concatenate([first[n, 0:ROWS] for n in sources], axis=0)
    found = jnp.dot(sent, face_pick[...], preferred_element_type=F32, precision=lax.Precision.HIGHEST)
    owner_rows = jnp.broadcast_to(owner, (ROWS, 128))
    right = jnp.zeros((ROWS, 128), F32)
    stab = jnp.zeros((ROWS, 128), F32)
    for at, n in enumerate(sources):
        block = found[at * ROWS : (at + 1) * ROWS]
        right = jnp.where(owner_rows == n, block[:, :128], right)
        stab = jnp.where(owner_rows == n, block[:, 128:], stab)
    scale = 1.0 / jnp.where(owner_rows >= 0, stab, 1.0)
    face_stab = pltpu.roll(first[SELF, 0:ROWS], 64, 1)
    face_scale = 1.0 / jnp.where(small < OWN * PARTS, face_stab, 1.0)

    def gathered(phase, width):
        stack = tiles[phase].reshape(KINDS * ROWS, 128)
        found = jnp.dot(stack, pick[:, 0:width], preferred_element_type=F32)
        kinds = kind_row[:, 0:width]
        total = []
        for begin in range(0, KINDS, 6):
            some = jnp.zeros((ROWS, width), F32)
            for n in range(begin, begin + 6):
                some = jnp.where(kinds == n, found[n * ROWS : (n + 1) * ROWS], some)
            total.append(some)
        return (total[0] + total[1]) + (total[2] + total[3])

    def face_sum(both):
        return both[:, 128:] + pltpu.roll(both[:, 128:], 64, 1)

    ones = [jnp.where(fourth == e, 1.0, 0.0).astype(BF16) for e in range(4)]

    def spread(lam):
        for k in range(6):
            for j in range(PARTS):
                block = jnp.take_along_axis(lam, fourth + (j * SLOTS + k * 4), axis=1).astype(BF16)
                begin = k * 80 + j * ROWS
                for e in range(4):
                    rhs_mat[e * 512 + begin : e * 512 + begin + ROWS] = block * ones[e]

    def image():
        product = jnp.dot(schur[...], rhs_mat[...], preferred_element_type=F32)
        tile = []
        for j in range(PARTS):
            some = jnp.zeros((ROWS, 128), F32)
            for k in range(6):
                place, begin = j * SLOTS + k * 4, k * 80 + j * ROWS
                fits = jnp.logical_and(small >= place, small < place + 4)
                some = jnp.where(fits, product[begin : begin + ROWS], some)
            tile.append(some)
        return (tile[0] + tile[1]) + (tile[2] + tile[3]) + tile[4]

    arrive(1, tiles.at[0], recv_sem)
    both = gathered(0, 256)
    right = right - (own + both[:, :128])
    face_right = first[SELF, 0:ROWS] - face_sum(both)
    spread(right * scale)
    for sweep in range(1, SWEEPS):
        own = image()
        tiles[sweep, SELF] = own.astype(BF16)
        send(sweep + 1, tiles.at[sweep])
        arrive(sweep + 1, tiles.at[sweep], recv_sem)
        both = gathered(sweep, 256 if sweep == SWEEPS - 1 else 128)
        spread((right + own + both[:, :128]) * scale)

    face_now = (face_right + face_sum(both)) * face_scale
    for j in range(PARTS):
        block = pltpu.roll(face_now, 128 - j * OWN, 1) if j else face_now
        square[j * ROWS : (j + 1) * ROWS] = block
    trace_out[...] = square[...].T[0:ROWS]
    back = jnp.dot(couple[...], rhs_mat[...], preferred_element_type=F32)
    back = jnp.concatenate([back, jnp.zeros((64, 128), F32)], axis=0)
    for n in range(3):
        columns = slice(n * 128, (n + 1) * 128)
        vol_out[:, columns] = local_rows[:, columns] - back[columns].T[0:8]

    arrive(0, first, send_sem)
    for phase in range(SWEEPS):
        arrive(phase + 1, tiles.at[phase], send_sem)


def write(trace_in, vol_in, trace_out, vol_out):
    trace_out[...] = trace_in[0:OWN, 0:80]
    vol_out[...] = vol_in[0:4, 0:320]


def solution(mesh):
    groups, members = mesh.shape["elem"], mesh.shape["face"]
    spec2, spec3 = P(("elem", "face"), None), P(("elem", "face"), None, None)

    def local(vol_inverse, vol_from_trace, trace_from_vol, vol_residual, face_ids, trace_residual, stabilization):
        vmem, hbm = pl.BlockSpec(memory_space=pltpu.VMEM), pl.BlockSpec(memory_space=pl.ANY)
        trace, vol = pl.pallas_call(
            functools.partial(kernel, groups, members),
            out_shape=(pltpu.VMEM((ROWS, 128), F32), pltpu.VMEM((8, 384), F32)),
            in_specs=[hbm] * 7,
            out_specs=(vmem, vmem),
            scratch_shapes=[
                pltpu.SMEM((4, 6), I32),
                pltpu.VMEM((4, 320), BF16),
                pltpu.VMEM((OWN, 80), F32),
                pltpu.VMEM((OWN, 80), F32),
                pltpu.VMEM((4, 320, 320), BF16),
                pltpu.VMEM((4, 320, 480), BF16),
                pltpu.VMEM((4, 320, 480), BF16),
                pltpu.VMEM((320, 2048), BF16),
                pltpu.VMEM((480, 2048), BF16),
                pltpu.VMEM((2048, 128), BF16),
                pltpu.VMEM((KINDS, ROWS + 8, 128), F32),
                pltpu.VMEM((SWEEPS, KINDS, ROWS, 128), BF16),
                pltpu.VMEM((128, 256), BF16),
                pltpu.VMEM((128, 256), F32),
                pltpu.VMEM((ROWS, 256), I32),
                pltpu.VMEM((128, 128), F32),
                pltpu.SemaphoreType.DMA((7,)),
                pltpu.SemaphoreType.DMA((SWEEPS + 1,)),
                pltpu.SemaphoreType.DMA((SWEEPS + 1,)),
            ],
            compiler_params=pltpu.CompilerParams(collective_id=0, has_side_effects=True),
            name="newton",
        )(
            face_ids, vol_inverse, vol_from_trace, jnp.swapaxes(trace_from_vol, 1, 2), vol_residual,
            trace_residual, stabilization,
        )
        return pl.pallas_call(
            write,
            out_shape=(
                jax.ShapeDtypeStruct(trace_residual.shape, F32),
                jax.ShapeDtypeStruct(vol_residual.shape, F32),
            ),
            in_specs=[vmem, vmem],
            out_specs=(vmem, vmem),
            name="write",
        )(pltpu.with_memory_space_constraint(trace, pltpu.VMEM), pltpu.with_memory_space_constraint(vol, pltpu.VMEM))

    return jax.shard_map(
        local,
        mesh=mesh,
        in_specs=(spec3, spec3, spec3, spec2, spec2, spec2, spec2),
        out_specs=(spec2, spec2),
        check_vma=False,
    )
```

time: 59.9 us -> 56.3 us (0.940)
  local copies, waits for them, and re-layouts: 5.12 us -> 0 us
  Pallas kernels: 53.9 us -> 55.6 us
    unnamed x3 -> x0, local copies, waits for them, and re-layouts: 5.12 us -> none
    pallas_call x1 -> x2, Pallas kernels: 53.9 us -> 55.6 us  [the longest x1 55 us: local(): pl.pallas_call(functools.partial(kernel, groups, members), out_shape=(plt...]
where the time goes in v2:
time: 56.3 us; the launch traced here: 56.2 us
  Pallas kernels  55.6 us (99%)
  between operations  0.64 us (1%)
    pallas_call x1, Pallas kernels, local(): pl.pallas_call(functools.partial(kernel, groups, members), out_shape=(plt...  55 us

profile of v2, /device:TPU:1, one launch (start us, length us, event | category | flops | bytes accessed | tf_op | source)
XLA Modules:
  0.0 56.2 jit_solution(12558741963073927874)
XLA Ops:
  0.6 55.0 %newton.1 = (f32[16,128]{1,0:T(8,128)S(1)}, f32[8,384]{1,0:T(8,128)S(1)}) custom-call(s32[4,6]{1,0:T(4,128)} %ids_hbm.1, bf16[4,320,320]{2,1,0:T(8,128)(2,1)} %inv_hbm.1, bf16[4,320,480]{2,1,0:T(8,128)(2,1)} %up_hbm.1, bf16[4,320,480]{2,1,0:T(8,128)(2,1)} %bitcast.1, bf16[4,320]{1,0:T(4,128)(2,1)} %vol_hbm.1, f32[12,80]{1,0:T(8,128)} %res_hbm.1, ...), custom_call_target="tpu_custom_call" | custom-call | tf_op jit(solution)/shard_map/newton/pallas_call | solution.py:279
  55.6 0.6 %write.1 = (f32[12,80]{1,0:T(8,128)}, f32[4,320]{1,0:T(4,128)}) custom-call(f32[16,128]{1,0:T(8,128)S(1)} %get-tuple-element.4.trace_in, f32[8,384]{1,0:T(8,128)S(1)} %get-tuple-element.5.vol_in), custom_call_target="tpu_custom_call" | custom-call | tf_op jit(solution)/shard_map/write/pallas_call | solution.py:311

commit v3 on v2

--- a/solution.py
+++ b/solution.py
@@ -48,8 +48,8 @@
     small = lax.broadcasted_iota(I32, (ROWS, 128), 1)
     low = lax.bitwise_and(small, 63)
     fourth = lax.bitwise_and(small, 3)
-    for e in range(4):
-        rhs_mat[e * 512 + 480 : (e + 1) * 512] = jnp.zeros((32, 128), BF16)
+    rhs_mat[480:512] = jnp.zeros((32, 128), BF16)
+    rhs_mat[992:1024] = jnp.zeros((32, 128), BF16)
 
     def send(phase, ref):
         for n, (shift, turn) in enumerate(PEERS):
@@ -102,6 +102,8 @@
     local = jnp.concatenate(
         [jnp.where(level == e, local[:, 0:320], 0.0).astype(BF16) for e in range(4)], axis=1
     )
+    pl.semaphore_wait(barrier, SELF)
+    send(0, first)
     loads[2].wait()
     load = jnp.zeros((ROWS, 480), F32)
     for e in range(4):
@@ -119,8 +121,6 @@
             own = jnp.where(jnp.logical_and(small >= place, small < place + 4), block, own)
     tiles[0, SELF] = own.astype(BF16)
 
-    pl.semaphore_wait(barrier, SELF)
-    send(0, first)
     send(1, tiles.at[0])
 
     loads[6].wait()
@@ -128,9 +128,8 @@
     def condense(e, carry):
         block = jnp.dot(inv[e], up[e], preferred_element_type=F32).astype(BF16)
         block = jnp.concatenate([block, jnp.zeros((320, 32), BF16)], axis=1)
-        columns = pl.ds(pl.multiple_of(e * 512, 512), 512)
-        couple[:, columns] = block
-        schur[:, columns] = lax.dot_general(
+        couple[e] = block
+        schur[e] = lax.dot_general(
             down[e], block, (((0,), (0,)), ((), ())), preferred_element_type=F32
         ).astype(BF16)
         return carry
@@ -184,10 +183,13 @@
         place = jnp.where(hit, offset, place)
     place = part[:, :128] * OWN + place
     slim = lax.broadcasted_iota(I32, (128, 128), 0)
-    face_pick[:, 0:128] = jnp.where(slim == place, 1.0, 0.0)
-    face_pick[:, 128:256] = jnp.where(slim == place + 64, 1.0, 0.0)
+    face_pick[:, 0:128] = jnp.where(slim == place, 1.0, 0.0).astype(BF16)
+    face_pick[:, 128:256] = jnp.where(slim == place + 64, 1.0, 0.0).astype(BF16)
     sent = jnp.concatenate([first[n, 0:ROWS] for n in sources], axis=0)
-    found = jnp.dot(sent, face_pick[...], preferred_element_type=F32, precision=lax.Precision.HIGHEST)
+    high = sent.astype(BF16)
+    rest = (sent - high.astype(F32)).astype(BF16)
+    found = jnp.dot(high, face_pick[...], preferred_element_type=F32)
+    found = found + jnp.dot(rest, face_pick[...], preferred_element_type=F32)
     owner_rows = jnp.broadcast_to(owner, (ROWS, 128))
     right = jnp.zeros((ROWS, 128), F32)
     stab = jnp.zeros((ROWS, 128), F32)
@@ -199,62 +201,74 @@
     face_stab = pltpu.roll(first[SELF, 0:ROWS], 64, 1)
     face_scale = 1.0 / jnp.where(small < OWN * PARTS, face_stab, 1.0)
 
-    def gathered(phase, width):
+    def gathered(phase, columns):
         stack = tiles[phase].reshape(KINDS * ROWS, 128)
-        found = jnp.dot(stack, pick[:, 0:width], preferred_element_type=F32)
-        kinds = kind_row[:, 0:width]
+        found = jnp.dot(stack, pick[:, columns], preferred_element_type=F32)
+        kinds = kind_row[:, columns]
         total = []
         for begin in range(0, KINDS, 6):
-            some = jnp.zeros((ROWS, width), F32)
+            some = jnp.zeros((ROWS, 128), F32)
             for n in range(begin, begin + 6):
                 some = jnp.where(kinds == n, found[n * ROWS : (n + 1) * ROWS], some)
             total.append(some)
         return (total[0] + total[1]) + (total[2] + total[3])
 
-    def face_sum(both):
-        return both[:, 128:] + pltpu.roll(both[:, 128:], 64, 1)
-
-    ones = [jnp.where(fourth == e, 1.0, 0.0).astype(BF16) for e in range(4)]
+    def partners(phase):
+        return gathered(phase, slice(0, 128))
+
+    def face_sum(phase):
+        both = gathered(phase, slice(128, 256))
+        return both + pltpu.roll(both, 64, 1)
+
+    def fits(place):
+        return jnp.logical_and(small >= place, small < place + 4)
+
+    odd = lax.bitwise_and(small, 1) == 1
 
     def spread(lam):
         for k in range(6):
             for j in range(PARTS):
-                block = jnp.take_along_axis(lam, fourth + (j * SLOTS + k * 4), axis=1).astype(BF16)
+                block = jnp.take_along_axis(lam, fourth + (j * SLOTS + k * 4), axis=1)
                 begin = k * 80 + j * ROWS
-                for e in range(4):
-                    rhs_mat[e * 512 + begin : e * 512 + begin + ROWS] = block * ones[e]
+                rhs_mat[begin : begin + ROWS] = jnp.where(odd, 0.0, block).astype(BF16)
+                rhs_mat[512 + begin : 512 + begin + ROWS] = jnp.where(odd, block, 0.0).astype(BF16)
+
+    def products(blocks):
+        left, right = (
+            jnp.dot(jnp.concatenate([blocks[e], blocks[e + 1]], axis=1), rhs_mat[...], preferred_element_type=F32)
+            for e in (0, 2)
+        )
+        return jnp.where(lax.bitwise_and(lax.broadcasted_iota(I32, left.shape, 1), 3) < 2, left, right)
 
     def image():
-        product = jnp.dot(schur[...], rhs_mat[...], preferred_element_type=F32)
+        product = products(schur)
         tile = []
         for j in range(PARTS):
             some = jnp.zeros((ROWS, 128), F32)
             for k in range(6):
-                place, begin = j * SLOTS + k * 4, k * 80 + j * ROWS
-                fits = jnp.logical_and(small >= place, small < place + 4)
-                some = jnp.where(fits, product[begin : begin + ROWS], some)
+                begin = k * 80 + j * ROWS
+                some = jnp.where(fits(j * SLOTS + k * 4), product[begin : begin + ROWS], some)
             tile.append(some)
         return (tile[0] + tile[1]) + (tile[2] + tile[3]) + tile[4]
 
     arrive(1, tiles.at[0], recv_sem)
-    both = gathered(0, 256)
-    right = right - (own + both[:, :128])
-    face_right = first[SELF, 0:ROWS] - face_sum(both)
+    right = right - (own + partners(0))
     spread(right * scale)
     for sweep in range(1, SWEEPS):
         own = image()
         tiles[sweep, SELF] = own.astype(BF16)
         send(sweep + 1, tiles.at[sweep])
+        if sweep == 1:
+            face_right = first[SELF, 0:ROWS] - face_sum(0)
         arrive(sweep + 1, tiles.at[sweep], recv_sem)
-        both = gathered(sweep, 256 if sweep == SWEEPS - 1 else 128)
-        spread((right + own + both[:, :128]) * scale)
-
-    face_now = (face_right + face_sum(both)) * face_scale
+        spread((right + own + partners(sweep)) * scale)
+
+    back = products(couple)
+    face_now = (face_right + face_sum(SWEEPS - 1)) * face_scale
     for j in range(PARTS):
         block = pltpu.roll(face_now, 128 - j * OWN, 1) if j else face_now
         square[j * ROWS : (j + 1) * ROWS] = block
     trace_out[...] = square[...].T[0:ROWS]
-    back = jnp.dot(couple[...], rhs_mat[...], preferred_element_type=F32)
     back = jnp.concatenate([back, jnp.zeros((64, 128), F32)], axis=0)
     for n in range(3):
         columns = slice(n * 128, (n + 1) * 128)
@@ -289,13 +303,13 @@
                 pltpu.VMEM((4, 320, 320), BF16),
                 pltpu.VMEM((4, 320, 480), BF16),
                 pltpu.VMEM((4, 320, 480), BF16),
-                pltpu.VMEM((320, 2048), BF16),
-                pltpu.VMEM((480, 2048), BF16),
-                pltpu.VMEM((2048, 128), BF16),
+                pltpu.VMEM((4, 320, 512), BF16),
+                pltpu.VMEM((4, 480, 512), BF16),
+                pltpu.VMEM((1024, 128), BF16),
                 pltpu.VMEM((KINDS, ROWS + 8, 128), F32),
                 pltpu.VMEM((SWEEPS, KINDS, ROWS, 128), BF16),
                 pltpu.VMEM((128, 256), BF16),
-                pltpu.VMEM((128, 256), F32),
+                pltpu.VMEM((128, 256), BF16),
                 pltpu.VMEM((ROWS, 256), I32),
                 pltpu.VMEM((128, 128), F32),
                 pltpu.SemaphoreType.DMA((7,)),

time: 56.3 us -> 53.8 us (0.956)
  Pallas kernels: 55.6 us -> 53 us
    pallas_call x1, Pallas kernels: 55 us -> 52.4 us  [local(): pl.pallas_call(functools.partial(kernel, groups, members), out_shape=(plt...]
where the time goes in v3:
time: 53.8 us; the launch traced here: 53.7 us
  Pallas kernels  53 us (99%)
  between operations  0.64 us (1%)
    pallas_call x1, Pallas kernels, local(): pl.pallas_call(functools.partial(kernel, groups, members), out_shape=(plt...  52.4 us

profile of v3, /device:TPU:1, one launch (start us, length us, event | category | flops | bytes accessed | tf_op | source)
XLA Modules:
  0.0 53.7 jit_solution(4666112659762756816)
XLA Ops:
  0.6 52.4 %newton.1 = (f32[16,128]{1,0:T(8,128)S(1)}, f32[8,384]{1,0:T(8,128)S(1)}) custom-call(s32[4,6]{1,0:T(4,128)} %ids_hbm.1, bf16[4,320,320]{2,1,0:T(8,128)(2,1)} %inv_hbm.1, bf16[4,320,480]{2,1,0:T(8,128)(2,1)} %up_hbm.1, bf16[4,320,480]{2,1,0:T(8,128)(2,1)} %bitcast.1, bf16[4,320]{1,0:T(4,128)(2,1)} %vol_hbm.1, f32[12,80]{1,0:T(8,128)} %res_hbm.1, ...), custom_call_target="tpu_custom_call" | custom-call | tf_op jit(solution)/shard_map/newton/pallas_call | solution.py:293
  53.1 0.6 %write.1 = (f32[12,80]{1,0:T(8,128)}, f32[4,320]{1,0:T(4,128)}) custom-call(f32[16,128]{1,0:T(8,128)S(1)} %get-tuple-element.4.trace_in, f32[8,384]{1,0:T(8,128)S(1)} %get-tuple-element.5.vol_in), custom_call_target="tpu_custom_call" | custom-call | tf_op jit(solution)/shard_map/write/pallas_call | solution.py:325

commit v4 on v3

--- a/solution.py
+++ b/solution.py
@@ -18,7 +18,7 @@
 
 
 def kernel(groups, members, ids_hbm, inv_hbm, up_hbm, down_hbm, vol_hbm, res_hbm, stab_hbm, trace_out, vol_out,
-           ids, vol_res, res_ref, stab_ref, inv, up, down, couple, schur, rhs_mat, first, tiles, pick, face_pick,
+           ids, vol_res, res_ref, stab_ref, inv, up, down, couple, schur, first, tiles, pick, face_pick,
            kind_row, square, load_sem, send_sem, recv_sem):
     group, member = lax.axis_index("elem"), lax.axis_index("face")
     group_faces = OWN * members
@@ -47,9 +47,47 @@
     used = inner < jnp.where(half, OWN * PARTS, SLOTS * PARTS)
     small = lax.broadcasted_iota(I32, (ROWS, 128), 1)
     low = lax.bitwise_and(small, 63)
-    fourth = lax.bitwise_and(small, 3)
-    rhs_mat[480:512] = jnp.zeros((32, 128), BF16)
-    rhs_mat[992:1024] = jnp.zeros((32, 128), BF16)
+    across_rows, across_lanes = lax.broadcasted_iota(I32, (8, 128), 0), lax.broadcasted_iota(I32, (8, 128), 1)
+    upper = across_rows < 4
+
+    def spot(k, j):
+        group = k * PARTS + j
+        return (j * 3 + k // 2) * 8, group // 8, group % 8 * ROWS
+
+    def to_rows(tile):
+        turned = jnp.concatenate([tile, jnp.zeros((112, 128), F32)], axis=0).T
+        rows = [jnp.zeros((8, 128), F32)] * 4
+        for k in range(6):
+            for j in range(PARTS):
+                begin, n, place = spot(k, j)
+                block = turned[begin : begin + 8]
+                block = pltpu.roll(block, place, 1) if place else block
+                here = jnp.logical_and(across_lanes >= place, across_lanes < place + ROWS)
+                here = jnp.logical_and(here, upper if k % 2 == 0 else across_rows >= 4)
+                rows[n] = jnp.where(here, block, rows[n])
+        rows = jnp.concatenate([row + pltpu.roll(row, 4, 0) for row in rows], axis=1)
+        return jnp.concatenate([rows, rows], axis=0).astype(BF16)
+
+    def to_tile(rows):
+        blocks = []
+        for j in range(PARTS):
+            for k in range(0, 6, 2):
+                pair = []
+                for odd in range(2):
+                    _, n, place = spot(k + odd, j)
+                    block = rows[:, n * 128 : (n + 1) * 128]
+                    pair.append(pltpu.roll(block, 128 - place, 1) if place else block)
+                blocks.append(jnp.where(upper, pair[0], pair[1]))
+        blocks.append(jnp.zeros((8, 128), F32))
+        return jnp.concatenate(blocks, axis=0).T[0:ROWS]
+
+    def products(rows, blocks):
+        total = jnp.dot(rows, blocks[0], preferred_element_type=F32)[0:8]
+        of = lax.bitwise_and(lax.broadcasted_iota(I32, total.shape, 0), 3)
+        for e in range(1, 4):
+            total = jnp.where(of == e, jnp.dot(rows, blocks[e], preferred_element_type=F32)[0:8], total)
+        return total
+
 
     def send(phase, ref):
         for n, (shift, turn) in enumerate(PEERS):
@@ -88,37 +126,25 @@
     first[SELF, ROWS : ROWS + 8] = jnp.broadcast_to(wanted_f[:, :128], (8, 128))
 
     loads[0].wait()
-    res_rows = jnp.concatenate([vol_res[...], jnp.zeros((124, 320), BF16)], axis=0)
+    res_rows = jnp.concatenate([vol_res[...], vol_res[...], jnp.zeros((120, 320), BF16)], axis=0)
     across = (((1,), (1,)), ((), ()))
     loads[1].wait()
     local = lax.dot_general(inv[0], res_rows, across, preferred_element_type=F32)
-    at = lax.broadcasted_iota(I32, local.shape, 1)
+    at = lax.bitwise_and(lax.broadcasted_iota(I32, local.shape, 1), 3)
     for e in range(1, 4):
         local = jnp.where(at == e, lax.dot_general(inv[e], res_rows, across, preferred_element_type=F32), local)
     local = jnp.concatenate([local, jnp.zeros((64, 128), F32)], axis=0)
     local = jnp.concatenate([local[n * 128 : (n + 1) * 128].T[0:ROWS] for n in range(3)], axis=1)
     local_rows = local[0:8]
-    level = lax.broadcasted_iota(I32, (ROWS, 320), 0)
-    local = jnp.concatenate(
-        [jnp.where(level == e, local[:, 0:320], 0.0).astype(BF16) for e in range(4)], axis=1
-    )
+    level = lax.bitwise_and(lax.broadcasted_iota(I32, (ROWS, 320), 0), 3)
     pl.semaphore_wait(barrier, SELF)
     send(0, first)
     loads[2].wait()
     load = jnp.zeros((ROWS, 480), F32)
     for e in range(4):
-        load = load + jnp.dot(local[:, e * 320 : (e + 1) * 320], down[e], preferred_element_type=F32)
-    load = jnp.concatenate([load, jnp.zeros((ROWS, 32), F32)], axis=1)
-    load = jnp.concatenate([load, jnp.zeros((112, 512), F32)], axis=0)
-    load = jnp.concatenate([load[:, n * 128 : (n + 1) * 128].T for n in range(4)], axis=0)
-    own = jnp.zeros((ROWS, 128), F32)
-    for j in range(PARTS):
-        for k in range(6):
-            begin = k * 80 + j * ROWS
-            place = j * SLOTS + k * 4
-            block = load[begin : begin + ROWS]
-            block = pltpu.roll(block, place, 1) if place else block
-            own = jnp.where(jnp.logical_and(small >= place, small < place + 4), block, own)
+        row = jnp.where(level == e, local[:, 0:320], 0.0).astype(BF16)
+        load = load + jnp.dot(row, down[e], preferred_element_type=F32)
+    own = to_tile(jnp.concatenate([load[0:8], jnp.zeros((8, 32), F32)], axis=1))
     tiles[0, SELF] = own.astype(BF16)
 
     send(1, tiles.at[0])
@@ -126,12 +152,11 @@
     loads[6].wait()
 
     def condense(e, carry):
-        block = jnp.dot(inv[e], up[e], preferred_element_type=F32).astype(BF16)
-        block = jnp.concatenate([block, jnp.zeros((320, 32), BF16)], axis=1)
+        block = lax.dot_general(up[e], inv[e], (((0,), (1,)), ((), ())), preferred_element_type=F32).astype(BF16)
+        block = jnp.concatenate([block, jnp.zeros((32, 320), BF16)], axis=0)
         couple[e] = block
-        schur[e] = lax.dot_general(
-            down[e], block, (((0,), (0,)), ((), ())), preferred_element_type=F32
-        ).astype(BF16)
+        block = jnp.dot(block, down[e], preferred_element_type=F32).astype(BF16)
+        schur[e] = jnp.concatenate([block, jnp.zeros((512, 32), BF16)], axis=1)
         return carry
 
     lax.fori_loop(0, 4, condense, 0)
@@ -220,59 +245,25 @@
         both = gathered(phase, slice(128, 256))
         return both + pltpu.roll(both, 64, 1)
 
-    def fits(place):
-        return jnp.logical_and(small >= place, small < place + 4)
-
-    odd = lax.bitwise_and(small, 1) == 1
-
-    def spread(lam):
-        for k in range(6):
-            for j in range(PARTS):
-                block = jnp.take_along_axis(lam, fourth + (j * SLOTS + k * 4), axis=1)
-                begin = k * 80 + j * ROWS
-                rhs_mat[begin : begin + ROWS] = jnp.where(odd, 0.0, block).astype(BF16)
-                rhs_mat[512 + begin : 512 + begin + ROWS] = jnp.where(odd, block, 0.0).astype(BF16)
-
-    def products(blocks):
-        left, right = (
-            jnp.dot(jnp.concatenate([blocks[e], blocks[e + 1]], axis=1), rhs_mat[...], preferred_element_type=F32)
-            for e in (0, 2)
-        )
-        return jnp.where(lax.bitwise_and(lax.broadcasted_iota(I32, left.shape, 1), 3) < 2, left, right)
-
-    def image():
-        product = products(schur)
-        tile = []
-        for j in range(PARTS):
-            some = jnp.zeros((ROWS, 128), F32)
-            for k in range(6):
-                begin = k * 80 + j * ROWS
-                some = jnp.where(fits(j * SLOTS + k * 4), product[begin : begin + ROWS], some)
-            tile.append(some)
-        return (tile[0] + tile[1]) + (tile[2] + tile[3]) + tile[4]
-
     arrive(1, tiles.at[0], recv_sem)
     right = right - (own + partners(0))
-    spread(right * scale)
+    rows = to_rows(right * scale)
     for sweep in range(1, SWEEPS):
-        own = image()
+        own = to_tile(products(rows, schur))
         tiles[sweep, SELF] = own.astype(BF16)
         send(sweep + 1, tiles.at[sweep])
         if sweep == 1:
             face_right = first[SELF, 0:ROWS] - face_sum(0)
         arrive(sweep + 1, tiles.at[sweep], recv_sem)
-        spread((right + own + partners(sweep)) * scale)
-
-    back = products(couple)
+        rows = to_rows((right + own + partners(sweep)) * scale)
+
+    back = products(rows, couple)
+    vol_out[...] = local_rows - jnp.concatenate([back, jnp.zeros((8, 64), F32)], axis=1)
     face_now = (face_right + face_sum(SWEEPS - 1)) * face_scale
     for j in range(PARTS):
         block = pltpu.roll(face_now, 128 - j * OWN, 1) if j else face_now
         square[j * ROWS : (j + 1) * ROWS] = block
     trace_out[...] = square[...].T[0:ROWS]
-    back = jnp.concatenate([back, jnp.zeros((64, 128), F32)], axis=0)
-    for n in range(3):
-        columns = slice(n * 128, (n + 1) * 128)
-        vol_out[:, columns] = local_rows[:, columns] - back[columns].T[0:8]
 
     arrive(0, first, send_sem)
     for phase in range(SWEEPS):
@@ -303,9 +294,8 @@
                 pltpu.VMEM((4, 320, 320), BF16),
                 pltpu.VMEM((4, 320, 480), BF16),
                 pltpu.VMEM((4, 320, 480), BF16),
-                pltpu.VMEM((4, 320, 512), BF16),
-                pltpu.VMEM((4, 480, 512), BF16),
-                pltpu.VMEM((1024, 128), BF16),
+                pltpu.VMEM((4, 512, 320), BF16),
+                pltpu.VMEM((4, 512, 512), BF16),
                 pltpu.VMEM((KINDS, ROWS + 8, 128), F32),
                 pltpu.VMEM((SWEEPS, KINDS, ROWS, 128), BF16),
                 pltpu.VMEM((128, 256), BF16),

time: 53.8 us -> 53.1 us (0.987)
  Pallas kernels: 53 us -> 52.3 us
    pallas_call x1, Pallas kernels: 52.4 us -> 51.7 us  [local(): pl.pallas_call(functools.partial(kernel, groups, members), out_shape=(plt...]
where the time goes in v4:
time: 53.1 us; the launch traced here: 53 us
  Pallas kernels  52.3 us (98%)
  between operations  0.64 us (1%)
    pallas_call x1, Pallas kernels, local(): pl.pallas_call(functools.partial(kernel, groups, members), out_shape=(plt...  51.7 us

profile of v4, /device:TPU:1, one launch (start us, length us, event | category | flops | bytes accessed | tf_op | source)
XLA Modules:
  0.0 53.0 jit_solution(10060362905551883127)
XLA Ops:
  0.6 51.7 %newton.1 = (f32[16,128]{1,0:T(8,128)S(1)}, f32[8,384]{1,0:T(8,128)S(1)}) custom-call(s32[4,6]{1,0:T(4,128)} %ids_hbm.1, bf16[4,320,320]{2,1,0:T(8,128)(2,1)} %inv_hbm.1, bf16[4,320,480]{2,1,0:T(8,128)(2,1)} %up_hbm.1, bf16[4,320,480]{2,1,0:T(8,128)(2,1)} %bitcast.1, bf16[4,320]{1,0:T(4,128)(2,1)} %vol_hbm.1, f32[12,80]{1,0:T(8,128)} %res_hbm.1, ...), custom_call_target="tpu_custom_call" | custom-call | tf_op jit(solution)/shard_map/newton/pallas_call | solution.py:284
  52.4 0.6 %write.1 = (f32[12,80]{1,0:T(8,128)}, f32[4,320]{1,0:T(4,128)}) custom-call(f32[16,128]{1,0:T(8,128)S(1)} %get-tuple-element.4.trace_in, f32[8,384]{1,0:T(8,128)S(1)} %get-tuple-element.5.vol_in), custom_call_target="tpu_custom_call" | custom-call | tf_op jit(solution)/shard_map/write/pallas_call | solution.py:315

commit v5 on v4

--- a/solution.py
+++ b/solution.py
@@ -14,6 +14,7 @@
 TURNS = (4, 3, 5, 2, 6, 1, 7)
 PEERS = tuple((1, i) for i in TURNS + (0,)) + tuple((-1, i) for i in TURNS + (0,)) + tuple((0, i) for i in TURNS)
 SELF = len(PEERS)
+FAR = 16
 KINDS = SELF + 1
 
 
@@ -95,14 +96,18 @@
                 src_ref=ref.at[SELF],
                 dst_ref=ref.at[n],
                 send_sem=send_sem.at[phase],
-                recv_sem=recv_sem.at[phase],
+                recv_sem=recv_sem.at[phase, int(n >= FAR)],
                 device_id=device(shift, turn),
                 device_id_type=MESH,
             ).start()
 
-    def arrive(phase, ref, sem):
+    def leave(phase, ref):
         some = ref.at[pl.ds(0, SELF)]
-        pltpu.make_async_copy(some, some, sem.at[phase]).wait()
+        pltpu.make_async_copy(some, some, send_sem.at[phase]).wait()
+
+    def arrive(phase, ref, near):
+        some = ref.at[pl.ds(FAR, SELF - FAR) if near else pl.ds(0, FAR)]
+        pltpu.make_async_copy(some, some, recv_sem.at[phase, near]).wait()
 
     loads[3].wait()
     own_base = group * group_faces + member * OWN
@@ -137,8 +142,6 @@
     local = jnp.concatenate([local[n * 128 : (n + 1) * 128].T[0:ROWS] for n in range(3)], axis=1)
     local_rows = local[0:8]
     level = lax.bitwise_and(lax.broadcasted_iota(I32, (ROWS, 320), 0), 3)
-    pl.semaphore_wait(barrier, SELF)
-    send(0, first)
     loads[2].wait()
     load = jnp.zeros((ROWS, 480), F32)
     for e in range(4):
@@ -147,6 +150,8 @@
     own = to_tile(jnp.concatenate([load[0:8], jnp.zeros((8, 32), F32)], axis=1))
     tiles[0, SELF] = own.astype(BF16)
 
+    pl.semaphore_wait(barrier, SELF)
+    send(0, first)
     send(1, tiles.at[0])
 
     loads[6].wait()
@@ -160,41 +165,6 @@
         return carry
 
     lax.fori_loop(0, 4, condense, 0)
-
-    arrive(0, first, recv_sem)
-    eight = lax.broadcasted_iota(I32, (8, 128), 0)
-    for base in range(0, KINDS, 8):
-        rows = jnp.zeros((8, 128), F32)
-        for n in range(8):
-            rows = jnp.where(eight == n, first[base + n, ROWS : ROWS + 8], rows)
-        square[base : base + 8] = rows
-    square[KINDS:32] = jnp.zeros((32 - KINDS, 128), F32)
-    held = square[...].T
-    slot_row = lax.broadcasted_iota(I32, (SLOTS, 128), 0).astype(F32)
-    wide_slot = jnp.broadcast_to(wanted_f[:, :128], (SLOTS, 128))
-    wide_face = jnp.broadcast_to(wanted_f[:, 128:], (SLOTS, 128))
-    slot_sum = jnp.zeros((SLOTS, 128), F32)
-    face_total = jnp.zeros((SLOTS, 128), F32)
-    least = jnp.full((SLOTS, 128), 4096.0, F32)
-    for n in range(KINDS):
-        column = jnp.broadcast_to(held[0:SLOTS, n : n + 1], (SLOTS, 128))
-        code = slot_row + 32.0 * n
-        slot_sum = slot_sum + jnp.where(column == wide_slot, code, 0.0)
-        if n < SELF and PEERS[n][0] > 0:
-            continue
-        hit = column == wide_face
-        face_total = face_total + jnp.where(hit, code, 0.0)
-        least = jnp.minimum(least, jnp.where(hit, code, 4096.0))
-    slot_sum = jnp.sum(slot_sum, axis=0, keepdims=True) - (SELF * 32 + index[:, :128]).astype(F32)
-    face_total = jnp.sum(face_total, axis=0, keepdims=True)
-    least = jnp.min(least, axis=0, keepdims=True)
-    face_code = jnp.where(lane[:, :128] < 64, least, face_total - least)
-    code = jnp.concatenate([slot_sum, face_code], axis=1).astype(I32)
-    kinds = jnp.where(used, lax.shift_right_arithmetic(code, 5), -1)
-    row = jnp.where(used, part * SLOTS + lax.bitwise_and(code, 31), -1)
-    deep = lax.broadcasted_iota(I32, (128, 256), 0)
-    pick[...] = jnp.where(deep == row, 1.0, 0.0).astype(BF16)
-    kind_row[...] = jnp.broadcast_to(kinds, (ROWS, 256))
 
     owner = jnp.full((1, 128), -1, I32)
     place = jnp.zeros((1, 128), I32)
@@ -210,43 +180,84 @@
     slim = lax.broadcasted_iota(I32, (128, 128), 0)
     face_pick[:, 0:128] = jnp.where(slim == place, 1.0, 0.0).astype(BF16)
     face_pick[:, 128:256] = jnp.where(slim == place + 64, 1.0, 0.0).astype(BF16)
-    sent = jnp.concatenate([first[n, 0:ROWS] for n in sources], axis=0)
-    high = sent.astype(BF16)
-    rest = (sent - high.astype(F32)).astype(BF16)
-    found = jnp.dot(high, face_pick[...], preferred_element_type=F32)
-    found = found + jnp.dot(rest, face_pick[...], preferred_element_type=F32)
     owner_rows = jnp.broadcast_to(owner, (ROWS, 128))
     right = jnp.zeros((ROWS, 128), F32)
     stab = jnp.zeros((ROWS, 128), F32)
-    for at, n in enumerate(sources):
-        block = found[at * ROWS : (at + 1) * ROWS]
-        right = jnp.where(owner_rows == n, block[:, :128], right)
-        stab = jnp.where(owner_rows == n, block[:, 128:], stab)
+
+    eight = lax.broadcasted_iota(I32, (8, 128), 0)
+    slot_row = lax.broadcasted_iota(I32, (SLOTS, 128), 0).astype(F32)
+    wide_slot = jnp.broadcast_to(wanted_f[:, :128], (SLOTS, 128))
+    wide_face = jnp.broadcast_to(wanted_f[:, 128:], (SLOTS, 128))
+    slot_sum = jnp.zeros((SLOTS, 128), F32)
+    face_total = jnp.zeros((SLOTS, 128), F32)
+    least = jnp.full((SLOTS, 128), 4096.0, F32)
+    for near in (1, 0):
+        arrive(0, first, near)
+        begin, end = (FAR, KINDS) if near else (0, FAR)
+        for base in range(begin, end, 8):
+            rows = jnp.zeros((8, 128), F32)
+            for n in range(8):
+                rows = jnp.where(eight == n, first[base + n, ROWS : ROWS + 8], rows)
+            square[base : base + 8] = rows
+        held = square[...].T
+        for n in range(begin, end):
+            column = jnp.broadcast_to(held[0:SLOTS, n : n + 1], (SLOTS, 128))
+            code = slot_row + 32.0 * n
+            slot_sum = slot_sum + jnp.where(column == wide_slot, code, 0.0)
+            if n < SELF and PEERS[n][0] > 0:
+                continue
+            hit = column == wide_face
+            face_total = face_total + jnp.where(hit, code, 0.0)
+            least = jnp.minimum(least, jnp.where(hit, code, 4096.0))
+        some = [n for n in sources if begin <= n < end]
+        sent = jnp.concatenate([first[n, 0:ROWS] for n in some], axis=0)
+        high = sent.astype(BF16)
+        rest = (sent - high.astype(F32)).astype(BF16)
+        found = jnp.dot(high, face_pick[...], preferred_element_type=F32)
+        found = found + jnp.dot(rest, face_pick[...], preferred_element_type=F32)
+        for at, n in enumerate(some):
+            block = found[at * ROWS : (at + 1) * ROWS]
+            right = jnp.where(owner_rows == n, block[:, :128], right)
+            stab = jnp.where(owner_rows == n, block[:, 128:], stab)
+    slot_sum = jnp.sum(slot_sum, axis=0, keepdims=True) - (SELF * 32 + index[:, :128]).astype(F32)
+    face_total = jnp.sum(face_total, axis=0, keepdims=True)
+    least = jnp.min(least, axis=0, keepdims=True)
+    face_code = jnp.where(lane[:, :128] < 64, least, face_total - least)
+    code = jnp.concatenate([slot_sum, face_code], axis=1).astype(I32)
+    kinds = jnp.where(used, lax.shift_right_arithmetic(code, 5), -1)
+    row = jnp.where(used, part * SLOTS + lax.bitwise_and(code, 31), -1)
+    deep = lax.broadcasted_iota(I32, (128, 256), 0)
+    pick[...] = jnp.where(deep == row, 1.0, 0.0).astype(BF16)
+    kind_row[...] = jnp.broadcast_to(kinds, (ROWS, 256))
     scale = 1.0 / jnp.where(owner_rows >= 0, stab, 1.0)
     face_stab = pltpu.roll(first[SELF, 0:ROWS], 64, 1)
     face_scale = 1.0 / jnp.where(small < OWN * PARTS, face_stab, 1.0)
 
-    def gathered(phase, columns):
-        stack = tiles[phase].reshape(KINDS * ROWS, 128)
+    def gathered(phase, columns, begin, end):
+        stack = tiles[phase, begin:end].reshape((end - begin) * ROWS, 128)
         found = jnp.dot(stack, pick[:, columns], preferred_element_type=F32)
         kinds = kind_row[:, columns]
         total = []
-        for begin in range(0, KINDS, 6):
+        for four in range(begin, end, 4):
             some = jnp.zeros((ROWS, 128), F32)
-            for n in range(begin, begin + 6):
-                some = jnp.where(kinds == n, found[n * ROWS : (n + 1) * ROWS], some)
+            for n in range(four, four + 4):
+                some = jnp.where(kinds == n, found[(n - begin) * ROWS : (n - begin + 1) * ROWS], some)
             total.append(some)
-        return (total[0] + total[1]) + (total[2] + total[3])
-
-    def partners(phase):
-        return gathered(phase, slice(0, 128))
+        while len(total) > 1:
+            total = [x + y for x, y in zip(total[::2], total[1::2])]
+        return total[0]
+
+    def partners(phase, known):
+        arrive(phase + 1, tiles.at[phase], 1)
+        known = known + gathered(phase, slice(0, 128), FAR, KINDS)
+        arrive(phase + 1, tiles.at[phase], 0)
+        return known + gathered(phase, slice(0, 128), 0, FAR)
 
     def face_sum(phase):
-        both = gathered(phase, slice(128, 256))
+        both = gathered(phase, slice(128, 256), FAR, KINDS) + gathered(phase, slice(128, 256), 0, FAR)
         return both + pltpu.roll(both, 64, 1)
 
-    arrive(1, tiles.at[0], recv_sem)
-    right = right - (own + partners(0))
+    right = right - partners(0, own)
     rows = to_rows(right * scale)
     for sweep in range(1, SWEEPS):
         own = to_tile(products(rows, schur))
@@ -254,8 +265,7 @@
         send(sweep + 1, tiles.at[sweep])
         if sweep == 1:
             face_right = first[SELF, 0:ROWS] - face_sum(0)
-        arrive(sweep + 1, tiles.at[sweep], recv_sem)
-        rows = to_rows((right + own + partners(sweep)) * scale)
+        rows = to_rows(partners(sweep, right + own) * scale)
 
     back = products(rows, couple)
     vol_out[...] = local_rows - jnp.concatenate([back, jnp.zeros((8, 64), F32)], axis=1)
@@ -265,9 +275,9 @@
         square[j * ROWS : (j + 1) * ROWS] = block
     trace_out[...] = square[...].T[0:ROWS]
 
-    arrive(0, first, send_sem)
+    leave(0, first)
     for phase in range(SWEEPS):
-        arrive(phase + 1, tiles.at[phase], send_sem)
+        leave(phase + 1, tiles.at[phase])
 
 
 def write(trace_in, vol_in, trace_out, vol_out):
@@ -304,7 +314,7 @@
                 pltpu.VMEM((128, 128), F32),
                 pltpu.SemaphoreType.DMA((7,)),
                 pltpu.SemaphoreType.DMA((SWEEPS + 1,)),
-                pltpu.SemaphoreType.DMA((SWEEPS + 1,)),
+                pltpu.SemaphoreType.DMA((SWEEPS + 1, 2)),
             ],
             compiler_params=pltpu.CompilerParams(collective_id=0, has_side_effects=True),
             name="newton",

time: 53.1 us -> 53.5 us (level)
  no operation moved by 1% of the time
where the time goes in v5:
time: 53.5 us; the launch traced here: 53.4 us
  Pallas kernels  52.7 us (99%)
  between operations  0.64 us (1%)
    pallas_call x1, Pallas kernels, local(): pl.pallas_call(functools.partial(kernel, groups, members), out_shape=(plt...  52.1 us

profile of v5, /device:TPU:1, one launch (start us, length us, event | category | flops | bytes accessed | tf_op | source)
XLA Modules:
  0.0 53.4 jit_solution(17027296452380430782)
XLA Ops:
  0.6 52.1 %newton.1 = (f32[16,128]{1,0:T(8,128)S(1)}, f32[8,384]{1,0:T(8,128)S(1)}) custom-call(s32[4,6]{1,0:T(4,128)} %ids_hbm.1, bf16[4,320,320]{2,1,0:T(8,128)(2,1)} %inv_hbm.1, bf16[4,320,480]{2,1,0:T(8,128)(2,1)} %up_hbm.1, bf16[4,320,480]{2,1,0:T(8,128)(2,1)} %bitcast.1, bf16[4,320]{1,0:T(4,128)(2,1)} %vol_hbm.1, f32[12,80]{1,0:T(8,128)} %res_hbm.1, ...), custom_call_target="tpu_custom_call" | custom-call | tf_op jit(solution)/shard_map/newton/pallas_call | solution.py:294
  52.7 0.6 %write.1 = (f32[12,80]{1,0:T(8,128)}, f32[4,320]{1,0:T(4,128)}) custom-call(f32[16,128]{1,0:T(8,128)S(1)} %get-tuple-element.4.trace_in, f32[8,384]{1,0:T(8,128)S(1)} %get-tuple-element.5.vol_in), custom_call_target="tpu_custom_call" | custom-call | tf_op jit(solution)/shard_map/write/pallas_call | solution.py:325
